TPU v7x, 512 devices: a whole 4x4x16 slice. The times are simulated.
512 devices in a mesh: row: 16 (over y, z_hi, core), col: 32 (over z_lo, x).
Axes of the slice: x: 4, y: 4, z: 16 (z_hi: 2, z_lo: 8; z = z_hi * 8 + z_lo), core: 2. Of those that a mesh axis runs over, the one named last changes fastest.
Arguments:
- images: bfloat16 [4096, 1024], P(('row', 'col')), may hold values from -6 to 6
- texts: bfloat16 [4096, 1024], P(('row', 'col')), may hold values from -6 to 6
- loss_weights: float32 [2], replicated, may hold values from 0.5 to 1.5
Outputs:
- grad_images: float32 [4096, 1024], P(('row', 'col'))
- grad_texts: float32 [4096, 1024], P(('row', 'col'))
All inputs are finite; a program needn't handle non-finite values.
Results may differ from a plain program's by a relative error of at most 0.0013.
Values may be sent and summed in bfloat16 or wider, within the bound.
A program may use at most 64 MiB of HBM per device.

v0:
```python
import math
import jax
import jax.numpy as jnp
from jax import lax
from jax.sharding import PartitionSpec as P


def local(images, texts, loss_weights):
    width = images.shape[1]
    batch = images.shape[0] * lax.axis_size("row") * lax.axis_size("col")
    scale = 1.0 / math.sqrt(width * batch)
    cross_scale = loss_weights[0] * scale
    inner_scale = loss_weights[1] * scale
    own = jnp.stack([images, texts])
    columns = lax.all_gather(own, "row", axis=1, tiled=True)
    col_img = columns[0]
    col_txt = columns[1]
    col_count = col_img.shape[0]
    keys = jnp.concatenate(
        [
            jnp.concatenate([col_txt, -col_img], axis=1),
            jnp.concatenate([col_img, -col_txt], axis=1),
        ],
        axis=0,
    )
    piece = lax.all_gather(own, "col", axis=1, tiled=True)
    joined = jnp.concatenate([piece[0], piece[1]], axis=1)
    scores = lax.dot_general(
        joined, keys, (((1,), (1,)), ((), ())), preferred_element_type=jnp.float32
    )
    p_mat = (scores[:, :col_count] * cross_scale).astype(jnp.bfloat16)
    q_mat = (scores[:, col_count:] * inner_scale).astype(jnp.bfloat16)
    joined, weights = (joined, jnp.concatenate([p_mat, q_mat], axis=1))
    result = jnp.dot(weights, keys, preferred_element_type=jnp.float32)
    terms = jnp.stack([result[:, :width], result[:, width:]])
    grads = lax.psum_scatter(terms, "col", scatter_dimension=1, tiled=True)
    return (grads[0], grads[1])


def solution(mesh):
    in_specs = (P(("row", "col"), None), P(("row", "col"), None), P())
    out_specs = (P(("row", "col"), None), P(("row", "col"), None))
    return jax.shard_map(local, mesh=mesh, in_specs=in_specs, out_specs=out_specs, check_vma=False)
```

profile of v0, /device:TPU:8, one launch (start us, length us, event | category | flops | bytes accessed | tf_op | source)
XLA Modules:
  0.0 497.0 jit_solution(4307591087020093460)
XLA Ops:
  7.2 0.0 all-gather.2.cloned.1.call-start
  7.2 1.4 pad_maximum_fusion.1
  8.6 0.0 all-gather.2.cloned.1.call-update
  8.6 0.0 reduce-scatter.2.cloned.1.call-start
  8.6 1.3 fusion.14
  11.2 54.2 %all_gather.7 = bf16[2,128,1024]{2,1,0:T(8,128)(2,1)S(1)} all-gather(bf16[2,8,1024]{2,1,0:T(8,128)(2,1)} %pad_maximum_fusion.1), channel_id=1, replica_groups=mesh['row'=16,'col'=32] {'row'}, dimensions={1}, use_global_device_ids=true | all-gather | bytes 557056 | tf_op jit(solution)/shard_map/all_gather | solution.py:15
  65.5 173.2 %all-gather.2.cloned.1.call-done = bf16[2,256,1024]{2,1,0:T(8,128)(2,1)} async-done(((bf16[2,8,1024]{2,1,0:T(8,128)(2,1)}), bf16[2,256,1024]{2,1,0:T(8,128)(2,1)}) %all-gather.2.cloned.1.call-update) | async-done | bytes 1048592 | tf_op jit(solution)/shard_map/all_gather | solution.py:26
  238.6 1.3 slice_bitcast_fusion.3
  239.9 0.6 fusion
  240.5 0.5 fusion.4
  241.0 0.2 slice_bitcast_fusion.1
  241.2 1.5 pad_maximum_fusion
  242.7 0.0 reduce-scatter.2.cloned.1.call-update
  242.7 246.1 %reduce-scatter.2.cloned.1.call-done = f32[2,8,1024]{2,1,0:T(8,128)} async-done(((f32[2,256,1024]{2,1,0:T(8,128)}), f32[2,8,1024]{2,1,0:T(8,128)}) %reduce-scatter.2.cloned.1.call-update) | async-done | bytes 65552 | tf_op jit(solution)/shard_map/reduce_scatter | solution.py:36
  488.8 1.4 slice_bitcast_fusion.6
  (3 shorter events, 0.1 us)
Async XLA Ops:
  7.2 231.5 %all-gather.2.cloned.1.call-start = ((), (), s32[]{:S(2)}) async-start(), calls=%async_computation.1 | async-start | bytes 1081344 | tf_op jit(solution)/shard_map/all_gather | solution.py:26
  8.6 480.2 %reduce-scatter.2.cloned.1.call-start = ((), (), s32[]{:S(2)}) async-start(), calls=%async_computation.2 | async-start | bytes 2162688 | tf_op jit(solution)/shard_map/reduce_scatter | solution.py:36
Sparse Core Ops, SparseCore 0:
  10.6 227.9 all-gather.1
  242.8 245.9 reduce-scatter.1
where the time goes:
time: 497 us
  waiting for transfers between devices  419 us (84%)
  blocking collectives  54.2 us (11%)
  between operations  15.3 us (3%)
    reduce_scatter x1, waiting for transfers between devices, local(): grads = lax.psum_scatter(terms, 'col', scatter_dimension=1, tiled=True)  246 us
    all_gather x1, waiting for transfers between devices, local(): piece = lax.all_gather(own, 'col', axis=1, tiled=True)  173 us
    all_gather x1, blocking collectives, local(): columns = lax.all_gather(own, 'row', axis=1, tiled=True)  54.2 us
  transfers between devices with their start and end apart: 2, of which 2 were waited for; matrix products, arithmetic and copies ran while one was open for 0% of the time, Pallas kernels for 0%

commit v1 on v0

--- a/solution.py
+++ b/solution.py
@@ -23,7 +23,9 @@
         ],
         axis=0,
     )
-    piece = lax.all_gather(own, "col", axis=1, tiled=True)
+    piece = jnp.concatenate(
+        lax.all_to_all(jnp.stack([own] * lax.axis_size("col")), "col", 0, 0), axis=1
+    )
     joined = jnp.concatenate([piece[0], piece[1]], axis=1)
     scores = lax.dot_general(
         joined, keys, (((1,), (1,)), ((), ())), preferred_element_type=jnp.float32

time: 497 us -> 366 us (0.74)
  waiting for transfers between devices: 419 us -> 276 us
  starting transfers between devices: 0.08 us -> 15.4 us
    all_gather x1 -> x0, waiting for transfers between devices: 173 us -> none  [local(): piece = lax.all_gather(own, 'col', axis=1, tiled=True)]
    reduce_scatter x1, waiting for transfers between devices: 246 us -> 263 us  [local(): grads = lax.psum_scatter(terms, 'col', scatter_dimension=1, tiled=True)]
    all_to_all x0 -> x1, starting transfers between devices: none -> 15.4 us  [local(): lax.all_to_all(jnp.stack([own] * lax.axis_size('col')), 'col', 0, 0)]
    all_to_all x0 -> x1, waiting for transfers between devices: none -> 13.6 us  [local(): lax.all_to_all(jnp.stack([own] * lax.axis_size('col')), 'col', 0, 0)]
where the time goes in v1:
time: 366 us; the launch traced here: 365 us
  waiting for transfers between devices  276 us (75%)
  blocking collectives  51.7 us (14%)
  starting transfers between devices  15.4 us (4%)
  between operations  15.4 us (4%)
    reduce_scatter x1, waiting for transfers between devices, local(): grads = lax.psum_scatter(terms, 'col', scatter_dimension=1, tiled=True)  263 us
    all_gather x1, blocking collectives, local(): columns = lax.all_gather(own, 'row', axis=1, tiled=True)  51.7 us
    all_to_all x1, starting transfers between devices, local(): lax.all_to_all(jnp.stack([own] * lax.axis_size('col')), 'col', 0, 0)  15.4 us
    all_to_all x1, waiting for transfers between devices, local(): lax.all_to_all(jnp.stack([own] * lax.axis_size('col')), 'col', 0, 0)  13.6 us
  transfers between devices with their start and end apart: 2, of which 2 were waited for; matrix products, arithmetic and copies ran while one was open for 0% of the time, Pallas kernels for 0%

profile of v1, /device:TPU:8, one launch (start us, length us, event | category | flops | bytes accessed | tf_op | source)
XLA Modules:
  0.0 365.5 jit_solution(17684801559719878337)
XLA Ops:
  7.2 0.0 copy-start
  7.2 0.7 pad_maximum_fusion.1
  7.9 1.1 stack.17
  9.0 15.4 %all-to-all-start = ((bf16[32,2,8,1024]{3,2,1,0:T(8,128)(2,1)}), bf16[32,2,8,1024]{3,2,1,0:T(8,128)(2,1)S(1)}, u32[]{:S(2)}, u32[]{:S(2)}) async-start(bf16[32,2,8,1024]{3,2,1,0:T(8,128)(2,1)} %stack.17), calls=%async_computation | async-start | bytes 2097152 | tf_op jit(solution)/shard_map/all_to_all | solution.py:27
  24.4 0.0 reduce-scatter.2.cloned.1.call-start
  24.5 0.0 copy-done
  24.5 0.6 fusion.14
  26.3 51.7 %all_gather.3 = bf16[2,128,1024]{2,1,0:T(8,128)(2,1)S(1)} all-gather(bf16[2,8,1024]{2,1,0:T(8,128)(2,1)S(1)} %pad_maximum_fusion.1), channel_id=1, replica_groups=mesh['row'=16,'col'=32] {'row'}, dimensions={1}, use_global_device_ids=true | all-gather | bytes 557056 | tf_op jit(solution)/shard_map/all_gather | solution.py:15
  78.1 13.6 %all-to-all-done = bf16[32,2,8,1024]{3,2,1,0:T(8,128)(2,1)S(1)} async-done(((bf16[32,2,8,1024]{3,2,1,0:T(8,128)(2,1)}), bf16[32,2,8,1024]{3,2,1,0:T(8,128)(2,1)S(1)}, u32[]{:S(2)}, u32[]{:S(2)}) %all-to-all-start) | async-done | bytes 1048608 | tf_op jit(solution)/shard_map/all_to_all | solution.py:27
  91.8 0.1 slice_bitcast_fusion.3
  91.8 0.6 fusion
  92.4 0.5 fusion.4
  92.9 0.1 slice_bitcast_fusion.1
  93.0 1.6 pad_maximum_fusion
  94.6 0.0 reduce-scatter.2.cloned.1.call-update
  94.7 262.6 %reduce-scatter.2.cloned.1.call-done = f32[2,8,1024]{2,1,0:T(8,128)} async-done(((f32[2,256,1024]{2,1,0:T(8,128)}), f32[2,8,1024]{2,1,0:T(8,128)}) %reduce-scatter.2.cloned.1.call-update) | async-done | bytes 65552 | tf_op jit(solution)/shard_map/reduce_scatter | solution.py:38
  357.2 1.4 slice_bitcast_fusion.6
  (3 shorter events, 0.1 us)
Async XLA Ops:
  7.2 17.3 %copy-start = (f32[2]{0:T(128)S(1)}, f32[2]{0:T(128)}, u32[]{:S(2)}) copy-start(f32[2]{0:T(128)} %param.5) | copy-start | bytes 28
  9.0 82.7 %all-to-all-start = ((bf16[32,2,8,1024]{3,2,1,0:T(8,128)(2,1)}), bf16[32,2,8,1024]{3,2,1,0:T(8,128)(2,1)S(1)}, u32[]{:S(2)}, u32[]{:S(2)}) async-start(bf16[32,2,8,1024]{3,2,1,0:T(8,128)(2,1)} %stack.17), calls=%async_computation | async-start | bytes 2097152 | tf_op jit(solution)/shard_map/all_to_all | solution.py:27
  24.4 332.8 %reduce-scatter.2.cloned.1.call-start = ((), (), s32[]{:S(2)}) async-start(), calls=%async_computation.2 | async-start | bytes 2162688 | tf_op jit(solution)/shard_map/reduce_scatter | solution.py:38
Sparse Core Ops, SparseCore 0:
  94.8 262.4 reduce-scatter.1
